TPU v7x, 32 devices: a whole 2x2x4 slice. The times are simulated.
32 devices in a mesh: grp: 2 (over y), tm: 8 (over z, x), space: 2 (over core).
Axes of the slice: x: 2, y: 2, z: 4, core: 2. Of those that a mesh axis runs over, the one named last changes fastest.
Arguments:
- tokens: bfloat16 [16, 24, 64, 1024], P(('grp', 'tm'), 'space'), parts along dimension 0, may hold values from -28 to 28
- gains: float32 [2, 1024], replicated, may hold values from 0.5 to 2
- qkv_weights: bfloat16 [2, 1024, 1536], replicated, may hold values from -1.125 to 1.125
- out_weights: bfloat16 [2, 512, 1024], replicated, may hold values from -0.25 to 0.25
Outputs:
- video_out: bfloat16 [16, 24, 64, 1024], P(('grp', 'tm'), 'space'), parts along dimension 0
There are 2 independent parts, one for each index of `grp`. A program takes and returns all parts, laid end to end along the dimension named above; an argument that names none is the same for every part. Nothing has to cross between parts.
All inputs are finite; a program needn't handle non-finite values.
Results may differ from a plain program's by a relative error of at most 0.007.
Values may be sent and summed in bfloat16 or wider, within the bound.
No kernel may reach another device: no remote copies, remote signals or barrier semaphores. Data moves between devices by JAX's collectives and lax.ppermute only.
A program may use at most 64 MiB of HBM per device.

v0:
```python
import jax
import jax.numpy as jnp
from jax import lax
from jax.sharding import PartitionSpec as P

HEADS = 8
HEAD = 64


def block_groups(groups, length):
    target = max(1, 512 // length)
    chosen = 1
    for candidate in range(1, min(groups, target) + 1):
        if groups % candidate == 0:
            chosen = candidate
    return chosen


def attend(tokens, length, gain_row, qkv_weight, out_weight):
    tok_count, feat_count = tokens.shape
    inner_width = out_weight.shape[0]
    stream = tokens.astype(jnp.float32)
    normed = (
        stream * lax.rsqrt(jnp.mean(stream * stream, axis=-1, keepdims=True) + 1e-06) * gain_row
    ).astype(jnp.bfloat16)
    projected = jnp.dot(normed, qkv_weight, preferred_element_type=jnp.float32).astype(jnp.bfloat16)
    per_block = block_groups(tok_count // length, length) * length
    blocks = tok_count // per_block
    shaped = projected.reshape(blocks, per_block, 3, HEADS, HEAD)
    scores = jnp.einsum(
        "bqhd,bkhd->bhqk", shaped[:, :, 0], shaped[:, :, 1], preferred_element_type=jnp.float32
    ) * HEAD ** (-0.5)
    group_ids = jnp.arange(per_block) // length
    same_group = group_ids[:, None] == group_ids[None, :]
    scores = jnp.where(same_group, scores, -1e30)
    row_max = jnp.max(scores, axis=-1, keepdims=True)
    raised = jnp.exp(scores - row_max)
    weights = (raised / jnp.sum(raised, axis=-1, keepdims=True)).astype(jnp.bfloat16)
    mixture = jnp.einsum(
        "bhqk,bkhd->bqhd", weights, shaped[:, :, 2], preferred_element_type=jnp.float32
    ).astype(jnp.bfloat16)
    mixture = mixture.reshape(tok_count, inner_width)
    update = jnp.dot(mixture, out_weight, preferred_element_type=jnp.float32)
    return (stream + update).astype(jnp.bfloat16)


def shards(tokens, gains, qkv_weights, out_weights):
    spread = lax.axis_size("space")
    frame_count = lax.axis_size("tm")
    frame_tokens = tokens[0]
    row_count, col_count, feat_count = frame_tokens.shape
    half_cols = col_count // spread
    transposed = jnp.transpose(frame_tokens, (1, 0, 2)).reshape(
        spread, half_cols, row_count, feat_count
    )
    piece = lax.all_to_all(transposed, "space", split_axis=0, concat_axis=2, tiled=True)
    col_items = piece.shape[1]
    height_n = piece.shape[2]
    flat = piece.reshape(col_items * height_n, feat_count)
    done = attend(flat, height_n, gains[0], qkv_weights[0], out_weights[0])
    columns_done = done.reshape(1, col_items, height_n, feat_count)
    regrouped = columns_done.reshape(half_cols, spread, row_count, feat_count).transpose(0, 2, 1, 3)
    span = col_count * row_count // frame_count
    regrouped = regrouped.reshape(frame_count, span, 1, feat_count)
    piece = lax.all_to_all(regrouped, "tm", split_axis=0, concat_axis=2, tiled=True)
    pos_items = piece.shape[1]
    frame_n = piece.shape[2]
    flat = piece.reshape(pos_items * frame_n, feat_count)
    done = attend(flat, frame_n, gains[1], qkv_weights[1], out_weights[1])
    timed = done.reshape(1, pos_items, frame_n, feat_count)
    paired = timed.reshape(span // spread, spread, frame_count, feat_count).transpose(0, 2, 1, 3)
    paired = paired.reshape(span // spread, frame_count * spread, feat_count)
    back_rows = lax.all_to_all(paired, ("tm", "space"), split_axis=1, concat_axis=0, tiled=True)
    back_rows = back_rows.reshape(frame_count, spread, span // spread, feat_count).transpose(
        1, 0, 2, 3
    )
    restored = back_rows.reshape(col_count, row_count, feat_count)
    return jnp.transpose(restored, (1, 0, 2))[None]


def solution(mesh):
    return jax.shard_map(
        shards,
        mesh=mesh,
        in_specs=(P(("grp", "tm"), "space", None, None), P(), P(), P()),
        out_specs=P(("grp", "tm"), "space", None, None),
        check_vma=False,
    )
```

profile of v0, /device:TPU:1, one launch (start us, length us, event | category | flops | bytes accessed | tf_op | source)
XLA Modules:
  0.0 207.1 jit_solution(540313732590014101)
XLA Ops:
  0.0 2.7 %copy.114 = bf16[2,32,12,1024]{3,1,2,0:T(8,128)(2,1)} copy(bf16[2,32,12,1024]{3,1,0,2:T(8,128)(2,1)} %bitcast.161) | data formatting | bytes 3145728 | tf_op jit(solution)/shard_map/reshape | solution.py:53
  2.7 3.8 %all-to-all-start = ((bf16[2,32,12,1024]{3,1,2,0:T(8,128)(2,1)}), bf16[2,32,12,1024]{3,1,2,0:T(8,128)(2,1)S(1)}, u32[]{:S(2)}, u32[]{:S(2)}) async-start(bf16[2,32,12,1024]{3,1,2,0:T(8,128)(2,1)} %copy.114), calls=%async_computation | async-start | bytes 3145728 | tf_op jit(solution)/shard_map/all_to_all | solution.py:56
  14.3 5.7 %convolution_convert_fusion.1 = bf16[768,1536]{1,0:T(8,128)(2,1)} fusion(bf16[768,1024]{1,0:T(8,128)(2,1)S(1)} %convert_element_type.84, bf16[2,1024,1536]{2,1,0:T(8,128)(2,1)} %param.6), kind=kOutput, calls=%fused_computation.23 | convolution fusion | flops 2417098752 | bytes 7077888 | tf_op jit(solution)/shard_map/dot_general | solution.py:26
  20.0 6.9 %reshape.162 = bf16[2,384,3,8,64]{4,3,2,1,0:T(8,128)(2,1)} reshape(bf16[768,1536]{1,0:T(8,128)(2,1)} %convolution_convert_fusion.1) | data formatting | bytes 4718592 | tf_op jit(solution)/shard_map/reshape | solution.py:29
  26.9 4.3 %fusion.75 = (bf16[2,384,1,8,64]{4,3,2,1,0:T(8,128)(2,1)S(1)}, bf16[2,384,1,8,64]{4,3,2,1,0:T(8,128)(2,1)}, bf16[2,384,1,8,64]{4,3,2,1,0:T(8,128)(2,1)}) fusion(bf16[2,384,3,8,64]{4,3,2,1,0:T(8,128)(2,1)} %reshape.162), kind=kLoop, calls=%fused_computation.86 | loop fusion | bytes 4718592 | tf_op jit(solution)/shard_map/slice | solution.py:40
  31.3 2.7 %copy.144 = bf16[2,384,1,8,64]{1,4,3,0,2:T(8,128)(2,1)} copy(bf16[2,384,1,8,64]{4,3,2,1,0:T(8,128)(2,1)} %get-tuple-element.9) | data formatting | bytes 1572864
  34.0 2.7 %copy.145 = bf16[2,384,1,8,64]{1,4,3,0,2:T(8,128)(2,1)} copy(bf16[2,384,1,8,64]{4,3,2,1,0:T(8,128)(2,1)} %get-tuple-element.10) | data formatting | bytes 1572864
  38.6 8.2 %fusion.77 = (f32[2,8,384]{2,1,0:T(8,128)S(1)}, f32[2,8,384,384]{2,3,1,0:T(8,128)}) fusion(pred[384,384]{0,1:T(8,128)(4,1)S(1)} %broadcast_compare_fusion.1, bf16[2,384,1,8,64]{1,4,3,0,2:T(8,128)(2,1)} %copy.145, bf16[2,384,1,8,64]{1,4,3,0,2:T(8,128)(2,1)} %copy.144), kind=kOutput, calls=%fused_computation.88 | convolution fusion | flops 311427456 | bytes 11182080 | tf_op jit(solution)/shard_map/sub | solution.py:37
  46.8 4.5 %fusion.30 = bf16[2,384,8,64]{1,3,2,0:T(8,128)(2,1)S(1)} fusion(f32[2,8,384,384]{2,3,1,0:T(8,128)} %get-tuple-element.14, f32[2,8,384]{2,1,0:T(8,128)S(1)} %get-tuple-element.13, bf16[2,384,1,8,64]{1,4,3,0,2:T(8,128)(2,1)S(1)} %copy-done), kind=kOutput, calls=%fused_computation.44 | convolution fusion | flops 307101696 | bytes 11034624 | tf_op jit(solution)/shard_map/bhqk,bkhd->bqhd/dot_general | solution.py:39
  53.5 3.8 %copy.115 = f32[1,32,2,12,1024]{4,3,2,1,0:T(8,128)} copy(f32[1,32,2,12,1024]{4,1,3,2,0:T(8,128)S(1)} %convert_bitcast_fusion.2) | data formatting | bytes 6291456 | tf_op jit(solution)/shard_map/convert_element_type | solution.py:22
  57.3 3.0 %reshape.156 = f32[768,1024]{1,0:T(8,128)S(1)} reshape(f32[1,32,2,12,1024]{4,3,2,1,0:T(8,128)} %copy.115) | data formatting | bytes 6291456 | tf_op jit(solution)/shard_map/convert_element_type | solution.py:22
  60.3 3.6 %add_convert_fusion = bf16[768,1024]{1,0:T(8,128)(2,1)} fusion(f32[768,1024]{1,0:T(8,128)S(1)} %reshape.156, bf16[768,512]{0,1:T(8,128)(2,1)} %bitcast.158, bf16[2,512,1024]{2,1,0:T(8,128)(2,1)} %param.7), kind=kOutput, calls=%fused_computation.33 | convolution fusion | flops 806879232 | bytes 6553600 | tf_op jit(solution)/shard_map/dot_general | solution.py:43
  66.5 2.8 %copy.123 = bf16[32,12,2,1024]{3,2,1,0:T(2,128)(2,1)} copy(bf16[32,12,2,1024]{3,1,2,0:T(8,128)(2,1)S(1)} %bitcast.153) | data formatting | bytes 3145728 | tf_op jit(solution)/shard_map/transpose | solution.py:62
  69.3 3.7 %reshape.150 = bf16[8,96,1,1024]{3,1,0,2:T(8,128)(2,1)} reshape(bf16[32,12,2,1024]{3,2,1,0:T(2,128)(2,1)} %copy.123) | data formatting | bytes 3145728 | tf_op jit(solution)/shard_map/reshape | solution.py:64
  72.9 7.0 %all-to-all-start.1 = ((bf16[8,96,1,1024]{3,1,2,0:T(8,128)(2,1)}), bf16[8,96,1,1024]{3,1,2,0:T(8,128)(2,1)S(1)}, u32[]{:S(2)}, u32[]{:S(2)}) async-start(bf16[8,96,1,1024]{3,1,2,0:T(8,128)(2,1)} %bitcast.14), calls=%async_computation.1 | async-start | bytes 3145728 | tf_op jit(solution)/shard_map/all_to_all | solution.py:65
  80.1 36.3 %all-to-all-done.1 = bf16[8,96,1,1024]{3,1,2,0:T(8,128)(2,1)S(1)} async-done(((bf16[8,96,1,1024]{3,1,2,0:T(8,128)(2,1)}), bf16[8,96,1,1024]{3,1,2,0:T(8,128)(2,1)S(1)}, u32[]{:S(2)}, u32[]{:S(2)}) %all-to-all-start.1) | async-done | bytes 1572896 | tf_op jit(solution)/shard_map/all_to_all | solution.py:65
  117.5 7.4 %convolution_convert_fusion = bf16[768,1536]{1,0:T(8,128)(2,1)} fusion(bf16[2,1024,1536]{2,1,0:T(8,128)(2,1)} %param.6, f32[1024]{0:T(1024)S(1)} %bitcast.165, f32[96,8]{1,0:T(8,128)S(1)} %copy.127, bf16[8,96,1,1024]{3,1,2,0:T(8,128)(2,1)S(1)} %all-to-all-done.1), kind=kOutput, calls=%fused_computation.22 | convolution fusion | flops 2420244480 | bytes 7085056 | tf_op jit(solution)/shard_map/dot_general | solution.py:26
  124.9 6.9 %reshape.163 = bf16[2,384,3,8,64]{4,3,2,1,0:T(8,128)(2,1)} reshape(bf16[768,1536]{1,0:T(8,128)(2,1)} %convolution_convert_fusion) | data formatting | bytes 4718592 | tf_op jit(solution)/shard_map/reshape | solution.py:29
  131.8 4.3 %fusion.74 = (bf16[2,384,1,8,64]{4,3,2,1,0:T(8,128)(2,1)S(1)}, bf16[2,384,1,8,64]{4,3,2,1,0:T(8,128)(2,1)}, bf16[2,384,1,8,64]{4,3,2,1,0:T(8,128)(2,1)}) fusion(bf16[2,384,3,8,64]{4,3,2,1,0:T(8,128)(2,1)} %reshape.163), kind=kLoop, calls=%fused_computation.85 | loop fusion | bytes 4718592 | tf_op jit(solution)/shard_map/slice | solution.py:40
  136.2 2.7 %copy.147 = bf16[2,384,1,8,64]{1,4,3,0,2:T(8,128)(2,1)} copy(bf16[2,384,1,8,64]{4,3,2,1,0:T(8,128)(2,1)} %get-tuple-element.6) | data formatting | bytes 1572864
  138.9 2.7 %copy.148 = bf16[2,384,1,8,64]{1,4,3,0,2:T(8,128)(2,1)} copy(bf16[2,384,1,8,64]{4,3,2,1,0:T(8,128)(2,1)} %get-tuple-element.7) | data formatting | bytes 1572864
  143.3 8.2 %fusion.86 = (f32[2,8,384]{2,1,0:T(8,128)S(1)}, f32[2,8,384,384]{2,3,1,0:T(8,128)}) fusion(pred[384,384]{0,1:T(8,128)(4,1)S(1)} %broadcast_compare_fusion, bf16[2,384,1,8,64]{1,4,3,0,2:T(8,128)(2,1)} %copy.148, bf16[2,384,1,8,64]{1,4,3,0,2:T(8,128)(2,1)} %copy.147), kind=kOutput, calls=%fused_computation.89 | convolution fusion | flops 311427456 | bytes 11182080 | tf_op jit(solution)/shard_map/sub | solution.py:37
  151.5 4.5 %fusion.31 = bf16[2,384,8,64]{1,3,2,0:T(8,128)(2,1)S(1)} fusion(f32[2,8,384,384]{2,3,1,0:T(8,128)} %get-tuple-element.16, f32[2,8,384]{2,1,0:T(8,128)S(1)} %get-tuple-element.15, bf16[2,384,1,8,64]{1,4,3,0,2:T(8,128)(2,1)S(1)} %copy-done.1), kind=kOutput, calls=%fused_computation.45 | convolution fusion | flops 307101696 | bytes 11034624 | tf_op jit(solution)/shard_map/bhqk,bkhd->bqhd/dot_general | solution.py:39
  160.0 41.4 %all_to_all.33 = bf16[48,16,1024]{2,0,1:T(8,128)(2,1)S(1)} all-to-all(bf16[48,16,1024]{2,0,1:T(8,128)(2,1)S(1)} %bitcast.155), channel_id=1, replica_groups=mesh['grp'=2,'tm'=8,'space'=2] {'tm','space'}, dimensions={1} | all-to-all | bytes 3145728 | tf_op jit(solution)/shard_map/all_to_all | solution.py:73
  (36 shorter events, 26.8 us)
Async XLA Ops:
  2.7 6.3 %copy-start.3 = (f32[2,1024]{1,0:T(2,128)S(1)}, f32[2,1024]{1,0:T(2,128)}, u32[]{:S(2)}) copy-start(f32[2,1024]{1,0:T(2,128)} %param.5) | copy-start | bytes 24580
  2.7 5.9 %all-to-all-start = ((bf16[2,32,12,1024]{3,1,2,0:T(8,128)(2,1)}), bf16[2,32,12,1024]{3,1,2,0:T(8,128)(2,1)S(1)}, u32[]{:S(2)}, u32[]{:S(2)}) async-start(bf16[2,32,12,1024]{3,1,2,0:T(8,128)(2,1)} %copy.114), calls=%async_computation | async-start | bytes 3145728 | tf_op jit(solution)/shard_map/all_to_all | solution.py:56
  38.5 8.2 %copy-start = (bf16[2,384,1,8,64]{1,4,3,0,2:T(8,128)(2,1)S(1)}, bf16[2,384,1,8,64]{1,4,3,0,2:T(8,128)(2,1)}, u32[]{:S(2)}) copy-start(bf16[2,384,1,8,64]{1,4,3,0,2:T(8,128)(2,1)} %copy.143) | copy-start | bytes 2359300
  72.9 43.5 %all-to-all-start.1 = ((bf16[8,96,1,1024]{3,1,2,0:T(8,128)(2,1)}), bf16[8,96,1,1024]{3,1,2,0:T(8,128)(2,1)S(1)}, u32[]{:S(2)}, u32[]{:S(2)}) async-start(bf16[8,96,1,1024]{3,1,2,0:T(8,128)(2,1)} %bitcast.14), calls=%async_computation.1 | async-start | bytes 3145728 | tf_op jit(solution)/shard_map/all_to_all | solution.py:65
  143.3 8.2 %copy-start.1 = (bf16[2,384,1,8,64]{1,4,3,0,2:T(8,128)(2,1)S(1)}, bf16[2,384,1,8,64]{1,4,3,0,2:T(8,128)(2,1)}, u32[]{:S(2)}) copy-start(bf16[2,384,1,8,64]{1,4,3,0,2:T(8,128)(2,1)} %copy.146) | copy-start | bytes 2359300
  156.0 1.6 copy-start.2
where the time goes:
time: 208 us; the launch traced here: 207 us
  local copies, waits for them, and re-layouts  70.2 us (34%)
  matrix products  43.7 us (21%)
  blocking collectives  41.4 us (20%)
  waiting for transfers between devices  38.4 us (18%)
  starting transfers between devices  10.8 us (5%)
  other arithmetic  2.39 us (1%)
    all_to_all x1, blocking collectives, shards(): lax.all_to_all(paired, ('tm', 'space'), split_axis=1, concat_axis=0, tile...  41.4 us
    all_to_all x1, waiting for transfers between devices, shards(): lax.all_to_all(regrouped, 'tm', split_axis=0, concat_axis=2, tiled=True)  36.3 us
    sub x2, matrix products, attend(): raised = jnp.exp(scores - row_max)  16.4 us
    unnamed x16, local copies, waits for them, and re-layouts  16 us
    reshape x2, local copies, waits for them, and re-layouts, attend(): shaped = projected.reshape(blocks, per_block, 3, HEADS, HEAD)  13.9 us
    dot_general x2, matrix products, attend(): jnp.dot(normed, qkv_weight, preferred_element_type=jnp.float32)  13.1 us
    dot_general x2, matrix products, attend(): jnp.einsum('bhqk,bkhd->bqhd', weights, shaped[:, :, 2], preferred_element...  9.06 us
    slice x2, local copies, waits for them, and re-layouts, attend(): shaped[:, :, 2]  8.7 us
  transfers between devices with their start and end apart: 2, of which 2 were waited for; matrix products, arithmetic and copies ran while one was open for 0% of the time, Pallas kernels for 0%

commit v1 on v0

--- a/solution.py
+++ b/solution.py
@@ -5,6 +5,18 @@
 
 HEADS = 8
 HEAD = 64
+
+
+def cut_along(shard, dim, length):
+    shape = shard.shape
+    blocks = shard.reshape(*shape[:dim], length, shape[dim] // length, *shape[dim + 1 :])
+    return jnp.moveaxis(blocks, dim, 0)
+
+
+def joined_along(tiles, dim):
+    tiles = jnp.moveaxis(tiles, 0, dim)
+    shape = tiles.shape
+    return tiles.reshape(*shape[:dim], shape[dim] * shape[dim + 1], *shape[dim + 2 :])
 
 
 def block_groups(groups, length):
@@ -62,7 +74,14 @@
     regrouped = columns_done.reshape(half_cols, spread, row_count, feat_count).transpose(0, 2, 1, 3)
     span = col_count * row_count // frame_count
     regrouped = regrouped.reshape(frame_count, span, 1, feat_count)
-    piece = lax.all_to_all(regrouped, "tm", split_axis=0, concat_axis=2, tiled=True)
+    size, mine = (lax.axis_size("tm"), lax.axis_index("tm"))
+    pieces = cut_along(regrouped, 0, size)
+    finished = [pieces[mine]]
+    for step in range(1, size):
+        sent = pieces[mine ^ step]
+        finished.append(lax.ppermute(sent, "tm", [(i, i ^ step) for i in range(size)]))
+    pieces = jnp.stack(finished)[mine ^ jnp.arange(size)]
+    piece = joined_along(pieces, 2)
     pos_items = piece.shape[1]
     frame_n = piece.shape[2]
     flat = piece.reshape(pos_items * frame_n, feat_count)

time: 208 us -> 201 us (0.966)
  waiting for transfers between devices: 38.4 us -> 22.6 us
  blocking collectives: 41.4 us -> 51.5 us
  local copies, waits for them, and re-layouts: 70.2 us -> 66.1 us
  starting transfers between devices: 10.8 us -> 14.7 us
  matrix products: 43.7 us -> 40.8 us
    all_to_all x1 -> x0, waiting for transfers between devices: 36.3 us -> none  [shards(): lax.all_to_all(regrouped, 'tm', split_axis=0, concat_axis=2, tiled=True)]
    ppermute x0 -> x7, waiting for transfers between devices: none -> 20.5 us  [shards(): lax.ppermute(sent, 'tm', [(i, i ^ step) for i in range(size)])]
    ppermute x0 -> x7, starting transfers between devices: none -> 10.9 us  [shards(): lax.ppermute(sent, 'tm', [(i, i ^ step) for i in range(size)])]
    all_to_all x1, blocking collectives: 41.4 us -> 51.5 us  [shards(): lax.all_to_all(paired, ('tm', 'space'), split_axis=1, concat_axis=0, tile...]
    all_to_all x1 -> x0, starting transfers between devices: 7 us -> none  [shards(): lax.all_to_all(regrouped, 'tm', split_axis=0, concat_axis=2, tiled=True)]
    reshape x1 -> x0, local copies, waits for them, and re-layouts: 3.66 us -> none  [shards(): regrouped = regrouped.reshape(frame_count, span, 1, feat_count)]
    sub x2, matrix products: 16.4 us -> 13.7 us  [attend(): raised = jnp.exp(scores - row_max)]
    another operation x0 -> x2, local copies, waits for them, and re-layouts: none -> 2.51 us  [the longest x1 2.5 us: cut_along(): shard.reshape(*shape[:dim], length, shape[dim] // length, *shape[dim + 1:])]
  transfers between devices with their start and end apart: 2 -> 8, of which waited for: 2 -> 6; matrix products, arithmetic and copies ran while one was open for 0% -> 0% of each run, Pallas kernels for 0% -> 0%
where the time goes in v1:
time: 201 us; the launch traced here: 200 us
  local copies, waits for them, and re-layouts  66.1 us (33%)
  blocking collectives  51.5 us (26%)
  matrix products  40.8 us (20%)
  waiting for transfers between devices  22.6 us (11%)
  starting transfers between devices  14.7 us (7%)
  other arithmetic  4.35 us (2%)
    all_to_all x1, blocking collectives, shards(): lax.all_to_all(paired, ('tm', 'space'), split_axis=1, concat_axis=0, tile...  51.5 us
    ppermute x7, waiting for transfers between devices, shards(): lax.ppermute(sent, 'tm', [(i, i ^ step) for i in range(size)])  20.5 us
    unnamed x28, local copies, waits for them, and re-layouts  15.4 us
    sub x2, matrix products, attend(): raised = jnp.exp(scores - row_max)  13.7 us
    dot_general x2, matrix products, attend(): jnp.dot(normed, qkv_weight, preferred_element_type=jnp.float32)  11.8 us
    reshape x2, local copies, waits for them, and re-layouts, attend(): shaped = projected.reshape(blocks, per_block, 3, HEADS, HEAD)  11.5 us
    ppermute x7, starting transfers between devices, shards(): lax.ppermute(sent, 'tm', [(i, i ^ step) for i in range(size)])  10.9 us
    dot_general x2, matrix products, attend(): jnp.einsum('bhqk,bkhd->bqhd', weights, shaped[:, :, 2], preferred_element...  9.21 us
  transfers between devices with their start and end apart: 8, of which 6 were waited for; matrix products, arithmetic and copies ran while one was open for 0% of the time, Pallas kernels for 0%

profile of v1, /device:TPU:1, one launch (start us, length us, event | category | flops | bytes accessed | tf_op | source)
XLA Modules:
  0.0 200.4 jit_solution(3263938845058010887)
XLA Ops:
  0.0 2.7 %copy.92 = bf16[2,32,12,1024]{3,1,2,0:T(8,128)(2,1)} copy(bf16[2,32,12,1024]{3,1,0,2:T(8,128)(2,1)} %bitcast.193) | data formatting | bytes 3145728 | tf_op jit(solution)/shard_map/reshape | solution.py:65
  2.7 3.8 %all-to-all-start = ((bf16[2,32,12,1024]{3,1,2,0:T(8,128)(2,1)}), bf16[2,32,12,1024]{3,1,2,0:T(8,128)(2,1)S(1)}, u32[]{:S(2)}, u32[]{:S(2)}) async-start(bf16[2,32,12,1024]{3,1,2,0:T(8,128)(2,1)} %copy.92), calls=%async_computation | async-start | bytes 3145728 | tf_op jit(solution)/shard_map/all_to_all | solution.py:68
  14.3 5.7 %convolution_convert_fusion.1 = bf16[768,1536]{1,0:T(8,128)(2,1)} fusion(bf16[768,1024]{1,0:T(8,128)(2,1)S(1)} %convert_element_type.80, bf16[2,1024,1536]{2,1,0:T(8,128)(2,1)} %param.6), kind=kOutput, calls=%fused_computation.20 | convolution fusion | flops 2417098752 | bytes 7077888 | tf_op jit(solution)/shard_map/dot_general | solution.py:38
  20.0 7.0 %reshape.183 = bf16[2,384,3,8,64]{4,3,2,1,0:T(8,128)(2,1)} reshape(bf16[768,1536]{1,0:T(8,128)(2,1)} %convolution_convert_fusion.1) | data formatting | bytes 4718592 | tf_op jit(solution)/shard_map/reshape | solution.py:41
  26.9 4.3 %fusion.66 = (bf16[2,384,1,8,64]{4,3,2,1,0:T(8,128)(2,1)S(1)}, bf16[2,384,1,8,64]{4,3,2,1,0:T(8,128)(2,1)}, bf16[2,384,1,8,64]{4,3,2,1,0:T(8,128)(2,1)}) fusion(bf16[2,384,3,8,64]{4,3,2,1,0:T(8,128)(2,1)} %reshape.183), kind=kLoop, calls=%fused_computation.98 | loop fusion | bytes 4718592 | tf_op jit(solution)/shard_map/slice | solution.py:52
  38.5 8.2 %fusion.68 = (f32[2,8,384]{2,1,0:T(8,128)S(1)}, f32[2,8,384,384]{2,3,1,0:T(8,128)}) fusion(pred[384,384]{0,1:T(8,128)(4,1)S(1)} %broadcast_compare_fusion.1, bf16[2,384,1,8,64]{1,4,3,0,2:T(8,128)(2,1)} %copy.128, bf16[2,384,1,8,64]{1,4,3,0,2:T(8,128)(2,1)} %copy.127), kind=kOutput, calls=%fused_computation.100 | convolution fusion | flops 311427456 | bytes 11182080 | tf_op jit(solution)/shard_map/sub | solution.py:49
  46.7 4.5 %fusion.21 = bf16[2,384,8,64]{1,3,2,0:T(8,128)(2,1)S(1)} fusion(f32[2,8,384,384]{2,3,1,0:T(8,128)} %get-tuple-element.22, f32[2,8,384]{2,1,0:T(8,128)S(1)} %get-tuple-element.21, bf16[2,384,1,8,64]{1,4,3,0,2:T(8,128)(2,1)S(1)} %copy-done.3), kind=kOutput, calls=%fused_computation.39 | convolution fusion | flops 307101696 | bytes 11034624 | tf_op jit(solution)/shard_map/bhqk,bkhd->bqhd/dot_general | solution.py:51
  53.5 3.8 %copy.93 = f32[1,32,2,12,1024]{4,3,2,1,0:T(8,128)} copy(f32[1,32,2,12,1024]{4,1,3,2,0:T(8,128)S(1)} %convert_bitcast_fusion.1) | data formatting | bytes 6291456 | tf_op jit(solution)/shard_map/convert_element_type | solution.py:34
  57.3 3.0 %reshape.162 = f32[768,1024]{1,0:T(8,128)S(1)} reshape(f32[1,32,2,12,1024]{4,3,2,1,0:T(8,128)} %copy.93) | data formatting | bytes 6291456 | tf_op jit(solution)/shard_map/convert_element_type | solution.py:34
  60.3 3.6 %add_convert_fusion = bf16[768,1024]{1,0:T(8,128)(2,1)} fusion(f32[768,1024]{1,0:T(8,128)S(1)} %reshape.162, bf16[768,512]{0,1:T(8,128)(2,1)} %bitcast.188, bf16[2,512,1024]{2,1,0:T(8,128)(2,1)} %param.7), kind=kOutput, calls=%fused_computation.30 | convolution fusion | flops 806879232 | bytes 6553600 | tf_op jit(solution)/shard_map/dot_general | solution.py:55
  66.4 2.8 %copy.101 = bf16[32,12,2,1024]{3,2,1,0:T(2,128)(2,1)} copy(bf16[32,12,2,1024]{3,1,2,0:T(8,128)(2,1)S(1)} %bitcast.182) | data formatting | bytes 3145728 | tf_op jit(solution)/shard_map/transpose | solution.py:74
  72.0 2.8 %collective-permute-start = (bf16[1,96,1,1024]{3,1,2,0:T(8,128)(2,1)S(1)}, bf16[1,96,1,1024]{3,1,2,0:T(8,128)(2,1)S(1)}, u32[]{:S(2)}, u32[]{:S(2)}) collective-permute-start(bf16[1,96,1,1024]{3,1,2,0:T(8,128)(2,1)S(1)} %get-tuple-element.17), channel_id=1, source_target_pairs={{0,2},{2,0},{4,6},{6,4},{8,10},{10,8},{12,14},{14,12},{1,3},{3,1},... | collective-permute-start | bytes 589832 | tf_op jit(solution)/shard_map/ppermute | solution.py:82
  79.6 3.4 %collective-permute-start.5 = (bf16[1,96,1,1024]{3,1,2,0:T(8,128)(2,1)S(1)}, bf16[1,96,1,1024]{3,1,2,0:T(8,128)(2,1)S(1)}, u32[]{:S(2)}, u32[]{:S(2)}) collective-permute-start(bf16[1,96,1,1024]{3,1,2,0:T(8,128)(2,1)S(1)} %get-tuple-element.12), channel_id=1, source_target_pairs={{0,12},{2,14},{4,8},{6,10},{8,4},{10,6},{12,0},{14,2},{1,13},{3,15... | collective-permute-start | bytes 589832 | tf_op jit(solution)/shard_map/ppermute | solution.py:82
  83.0 5.1 %collective-permute-done.1 = bf16[1,96,1,1024]{3,1,2,0:T(8,128)(2,1)S(1)} collective-permute-done((bf16[1,96,1,1024]{3,1,2,0:T(8,128)(2,1)S(1)}, bf16[1,96,1,1024]{3,1,2,0:T(8,128)(2,1)S(1)}, u32[]{:S(2)}, u32[]{:S(2)}) %collective-permute-start.1) | collective-permute-done | bytes 196640 | tf_op jit(solution)/shard_map/ppermute | solution.py:82
  88.1 3.7 %collective-permute-done.2 = bf16[1,96,1,1024]{3,1,2,0:T(8,128)(2,1)S(1)} collective-permute-done((bf16[1,96,1,1024]{3,1,2,0:T(8,128)(2,1)S(1)}, bf16[1,96,1,1024]{3,1,2,0:T(8,128)(2,1)S(1)}, u32[]{:S(2)}, u32[]{:S(2)}) %collective-permute-start.2) | collective-permute-done | bytes 196640 | tf_op jit(solution)/shard_map/ppermute | solution.py:82
  92.3 7.1 %collective-permute-done.5 = bf16[1,96,1,1024]{3,1,2,0:T(8,128)(2,1)S(1)} collective-permute-done((bf16[1,96,1,1024]{3,1,2,0:T(8,128)(2,1)S(1)}, bf16[1,96,1,1024]{3,1,2,0:T(8,128)(2,1)S(1)}, u32[]{:S(2)}, u32[]{:S(2)}) %collective-permute-start.5) | collective-permute-done | bytes 196640 | tf_op jit(solution)/shard_map/ppermute | solution.py:82
  99.5 4.2 %collective-permute-done.6 = bf16[1,96,1,1024]{3,1,2,0:T(8,128)(2,1)S(1)} collective-permute-done((bf16[1,96,1,1024]{3,1,2,0:T(8,128)(2,1)S(1)}, bf16[1,96,1,1024]{3,1,2,0:T(8,128)(2,1)S(1)}, u32[]{:S(2)}, u32[]{:S(2)}) %collective-permute-start.6) | collective-permute-done | bytes 196640 | tf_op jit(solution)/shard_map/ppermute | solution.py:82
  107.2 6.1 %convolution_convert_fusion = bf16[768,1536]{1,0:T(8,128)(2,1)S(1)} fusion(bf16[2,1024,1536]{2,1,0:T(8,128)(2,1)} %param.6, bf16[1,96,8,1,1024]{4,1,2,3,0:T(8,128)(2,1)S(1)} %multiply_convert_fusion), kind=kOutput, calls=%fused_computation.19 | convolution fusion | flops 2417098752 | bytes 7077888 | tf_op jit(solution)/shard_map/dot_general | solution.py:38
  113.3 4.5 %reshape.184 = bf16[2,384,3,8,64]{4,3,2,1,0:T(8,128)(2,1)} reshape(bf16[768,1536]{1,0:T(8,128)(2,1)S(1)} %convolution_convert_fusion) | data formatting | bytes 4718592 | tf_op jit(solution)/shard_map/reshape | solution.py:41
  117.8 3.8 %fusion.65 = (bf16[2,384,1,8,64]{4,3,2,1,0:T(8,128)(2,1)S(1)}, bf16[2,384,1,8,64]{4,3,2,1,0:T(8,128)(2,1)}, bf16[2,384,1,8,64]{4,3,2,1,0:T(8,128)(2,1)S(1)}) fusion(bf16[2,384,3,8,64]{4,3,2,1,0:T(8,128)(2,1)} %reshape.184), kind=kLoop, calls=%fused_computation.97 | loop fusion | bytes 4718592 | tf_op jit(solution)/shard_map/slice | solution.py:52
  121.6 2.7 %copy.130 = bf16[2,384,1,8,64]{1,4,3,0,2:T(8,128)(2,1)} copy(bf16[2,384,1,8,64]{4,3,2,1,0:T(8,128)(2,1)} %get-tuple-element.6) | data formatting | bytes 1572864
  127.7 5.5 %fusion.77 = (f32[2,8,384]{2,1,0:T(8,128)S(1)}, f32[2,8,384,384]{2,3,1,0:T(8,128)}) fusion(pred[384,384]{0,1:T(8,128)(4,1)S(1)} %broadcast_compare_fusion, bf16[2,384,1,8,64]{1,4,3,0,2:T(8,128)(2,1)S(1)} %copy-done.4, bf16[2,384,1,8,64]{1,4,3,0,2:T(8,128)(2,1)S(1)} %copy-done.2), kind=kOutput, calls=%fused_computation.101 | convolution fusion | flops 311427456 | bytes 11182080 | tf_op jit(solution)/shard_map/sub | solution.py:49
  133.3 4.7 %fusion.22 = bf16[2,384,8,64]{1,3,2,0:T(8,128)(2,1)S(1)} fusion(f32[2,8,384,384]{2,3,1,0:T(8,128)} %get-tuple-element.24, f32[2,8,384]{2,1,0:T(8,128)S(1)} %get-tuple-element.23, bf16[2,384,1,8,64]{1,4,3,0,2:T(8,128)(2,1)S(1)} %copy-done.5), kind=kOutput, calls=%fused_computation.40 | convolution fusion | flops 307101696 | bytes 11034624 | tf_op jit(solution)/shard_map/bhqk,bkhd->bqhd/dot_general | solution.py:51
  143.2 51.5 %all_to_all.24 = bf16[48,16,1024]{2,0,1:T(8,128)(2,1)S(1)} all-to-all(bf16[48,16,1024]{2,0,1:T(8,128)(2,1)S(1)} %bitcast.184), channel_id=1, replica_groups=mesh['grp'=2,'tm'=8,'space'=2] {'tm','space'}, dimensions={1} | all-to-all | bytes 3145728 | tf_op jit(solution)/shard_map/all_to_all | solution.py:92
  (64 shorter events, 45.5 us)
Async XLA Ops:
  2.7 6.3 %copy-start.6 = (f32[2,1024]{1,0:T(2,128)S(1)}, f32[2,1024]{1,0:T(2,128)}, u32[]{:S(2)}) copy-start(f32[2,1024]{1,0:T(2,128)} %param.5) | copy-start | bytes 24580
  2.7 5.9 %all-to-all-start = ((bf16[2,32,12,1024]{3,1,2,0:T(8,128)(2,1)}), bf16[2,32,12,1024]{3,1,2,0:T(8,128)(2,1)S(1)}, u32[]{:S(2)}, u32[]{:S(2)}) async-start(bf16[2,32,12,1024]{3,1,2,0:T(8,128)(2,1)} %copy.92), calls=%async_computation | async-start | bytes 3145728 | tf_op jit(solution)/shard_map/all_to_all | solution.py:68
  38.5 8.2 %copy-start.3 = (bf16[2,384,1,8,64]{1,4,3,0,2:T(8,128)(2,1)S(1)}, bf16[2,384,1,8,64]{1,4,3,0,2:T(8,128)(2,1)}, u32[]{:S(2)}) copy-start(bf16[2,384,1,8,64]{1,4,3,0,2:T(8,128)(2,1)} %copy.126) | copy-start | bytes 2359300
  72.0 7.7 %collective-permute-start = (bf16[1,96,1,1024]{3,1,2,0:T(8,128)(2,1)S(1)}, bf16[1,96,1,1024]{3,1,2,0:T(8,128)(2,1)S(1)}, u32[]{:S(2)}, u32[]{:S(2)}) collective-permute-start(bf16[1,96,1,1024]{3,1,2,0:T(8,128)(2,1)S(1)} %get-tuple-element.17), channel_id=1, source_target_pairs={{0,2},{2,0},{4,6},{6,4},{8,10},{10,8},{12,14},{14,12},{1,3},{3,1},... | collective-permute-start | bytes 589832 | tf_op jit(solution)/shard_map/ppermute | solution.py:82
  74.7 13.4 %collective-permute-start.1 = (bf16[1,96,1,1024]{3,1,2,0:T(8,128)(2,1)S(1)}, bf16[1,96,1,1024]{3,1,2,0:T(8,128)(2,1)S(1)}, u32[]{:S(2)}, u32[]{:S(2)}) collective-permute-start(bf16[1,96,1,1024]{3,1,2,0:T(8,128)(2,1)S(1)} %get-tuple-element.16), channel_id=1, source_target_pairs={{0,4},{2,6},{4,0},{6,2},{8,12},{10,14},{12,8},{14,10},{1,5},{3,7},... | collective-permute-start | bytes 589832 | tf_op jit(solution)/shard_map/ppermute | solution.py:82
  76.0 15.8 %collective-permute-start.2 = (bf16[1,96,1,1024]{3,1,2,0:T(8,128)(2,1)S(1)}, bf16[1,96,1,1024]{3,1,2,0:T(8,128)(2,1)S(1)}, u32[]{:S(2)}, u32[]{:S(2)}) collective-permute-start(bf16[1,96,1,1024]{3,1,2,0:T(8,128)(2,1)S(1)} %get-tuple-element.15), channel_id=1, source_target_pairs={{0,6},{2,4},{4,2},{6,0},{8,14},{10,12},{12,10},{14,8},{1,7},{3,5},... | collective-permute-start | bytes 589832 | tf_op jit(solution)/shard_map/ppermute | solution.py:82
  76.0 15.8 %collective-permute-start.3 = (bf16[1,96,1,1024]{3,1,2,0:T(8,128)(2,1)S(1)}, bf16[1,96,1,1024]{3,1,2,0:T(8,128)(2,1)S(1)}, u32[]{:S(2)}, u32[]{:S(2)}) collective-permute-start(bf16[1,96,1,1024]{3,1,2,0:T(8,128)(2,1)S(1)} %get-tuple-element.14), channel_id=1, source_target_pairs={{0,8},{2,10},{4,12},{6,14},{8,0},{10,2},{12,4},{14,6},{1,9},{3,11}... | collective-permute-start | bytes 589832 | tf_op jit(solution)/shard_map/ppermute | solution.py:82
  78.5 13.8 %collective-permute-start.4 = (bf16[1,96,1,1024]{3,1,2,0:T(8,128)(2,1)S(1)}, bf16[1,96,1,1024]{3,1,2,0:T(8,128)(2,1)S(1)}, u32[]{:S(2)}, u32[]{:S(2)}) collective-permute-start(bf16[1,96,1,1024]{3,1,2,0:T(8,128)(2,1)S(1)} %get-tuple-element.13), channel_id=1, source_target_pairs={{0,10},{2,8},{4,14},{6,12},{8,2},{10,0},{12,6},{14,4},{1,11},{3,9}... | collective-permute-start | bytes 589832 | tf_op jit(solution)/shard_map/ppermute | solution.py:82
  79.6 19.8 %collective-permute-start.5 = (bf16[1,96,1,1024]{3,1,2,0:T(8,128)(2,1)S(1)}, bf16[1,96,1,1024]{3,1,2,0:T(8,128)(2,1)S(1)}, u32[]{:S(2)}, u32[]{:S(2)}) collective-permute-start(bf16[1,96,1,1024]{3,1,2,0:T(8,128)(2,1)S(1)} %get-tuple-element.12), channel_id=1, source_target_pairs={{0,12},{2,14},{4,8},{6,10},{8,4},{10,6},{12,0},{14,2},{1,13},{3,15... | collective-permute-start | bytes 589832 | tf_op jit(solution)/shard_map/ppermute | solution.py:82
  88.1 15.5 %collective-permute-start.6 = (bf16[1,96,1,1024]{3,1,2,0:T(8,128)(2,1)S(1)}, bf16[1,96,1,1024]{3,1,2,0:T(8,128)(2,1)S(1)}, u32[]{:S(2)}, u32[]{:S(2)}) collective-permute-start(bf16[1,96,1,1024]{3,1,2,0:T(8,128)(2,1)S(1)} %get-tuple-element.11), channel_id=1, source_target_pairs={{0,14},{2,12},{4,10},{6,8},{8,6},{10,4},{12,2},{14,0},{1,15},{3,13... | collective-permute-start | bytes 589832 | tf_op jit(solution)/shard_map/ppermute | solution.py:82
  126.0 1.7 copy-start.2
  126.0 1.7 copy-start.4
  127.7 5.5 %copy-start.5 = (bf16[2,384,1,8,64]{1,4,3,0,2:T(8,128)(2,1)S(1)}, bf16[2,384,1,8,64]{1,4,3,0,2:T(8,128)(2,1)}, u32[]{:S(2)}) copy-start(bf16[2,384,1,8,64]{1,4,3,0,2:T(8,128)(2,1)} %copy.129) | copy-start | bytes 2359300
  133.3 5.7 %copy-start.1 = (bf16[2,512,1024]{2,1,0:T(8,128)(2,1)S(1)}, bf16[2,512,1024]{2,1,0:T(8,128)(2,1)}, u32[]{:S(2)}) copy-start(bf16[2,512,1024]{2,1,0:T(8,128)(2,1)} %param.7) | copy-start | bytes 6291460
  138.0 1.9 copy-start
